TPU v7x, 128 devices: a whole 4x4x4 slice. The times are simulated.
128 devices in a mesh: ctx: 32 (over y, z, core), exp: 4 (over x).
Axes of the slice: x: 4, y: 4, z: 4, core: 2. Of those that a mesh axis runs over, the one named last changes fastest.
Arguments:
- stream_in: bfloat16 [4096, 6144], P('ctx'), may hold values from -41 to 41
- queries: bfloat16 [4096, 8192], P('ctx', 'exp'), may hold values from -6 to 6
- key_proj: bfloat16 [4096, 8192], P('ctx', 'exp'), may hold values from -0.5390625 to 0.5390625
- values: bfloat16 [4096, 8192], P('ctx', 'exp'), may hold values from -6 to 6
- attn_gate: bfloat16 [4096, 8192], P('ctx', 'exp'), may hold values from -6 to 6
- decay_rates: float32 [64], P('exp'), may hold values from 1.2207031e-05 to 0.05
- attn_gain: float32 [8192], P('exp'), may hold values from 0.25 to 1.75
- out_weight: bfloat16 [8192, 6144], P('exp', 'ctx'), may hold values from -0.0625 to 0.0625
- ffn_gain: float32 [6144], replicated, may hold values from 0.25 to 1.75
- routing: int32 [4096, 2], P('ctx'), may hold values from 0 to 31, as said below
- route_weights: float32 [4096, 2], P('ctx'), may hold values from 0.25 to 1
- w_gate: bfloat16 [4, 6144, 9216], P('exp', None, 'ctx'), may hold values from -0.078125 to 0.078125
- w_up: bfloat16 [4, 6144, 9216], P('exp', None, 'ctx'), may hold values from -0.078125 to 0.078125
- w_down: bfloat16 [4, 9216, 6144], P('exp', 'ctx'), may hold values from -0.0625 to 0.0625
Outputs:
- residual_out: bfloat16 [4096, 6144], P(('ctx', 'exp'))
- expert_out: bfloat16 [32, 4, 8, 6144], P('ctx', 'exp')
Inputs may be any that keep to these rules, and one draw needn't show every extreme that they name: `routing`: the two ids of a row differ and at most one of them is below 4. In each aligned block of 128 rows (one context shard) an id below 4 is named by at most 8 rows; one such id, the same for all blocks, is named by exactly 8 rows in every block.
All inputs are finite; a program needn't handle non-finite values.
Results may differ from a plain program's by a relative error of at most 0.025.
Values may be sent and summed in bfloat16 or wider, within the bound.
A program may use at most 128 MiB of HBM per device.

v0:
```python
import jax
import jax.numpy as jnp
from jax import lax
from jax.sharding import PartitionSpec as P

HIGHEST = lax.Precision.HIGHEST
CTX = ("yz", "core")


def decayed_prefix(local_state, decay_rates, rows_here):
    count = lax.axis_size(CTX)

    def shift(value, step):
        pairs = [(i, i + step) for i in range(count - step)]
        return lax.ppermute(value.astype(jnp.bfloat16), CTX, pairs).astype(jnp.float32)

    running = shift(local_state, 1)
    step = 1
    while step < count:
        factor = jnp.exp(-decay_rates * (rows_here * step))
        running = running + factor[:, None, None] * shift(running, step)
        step *= 2
    return running


def normalize_rows(row_block, ffn_gain):
    wide_rows = row_block.astype(jnp.float32)
    inverse = lax.rsqrt(jnp.mean(wide_rows * wide_rows, axis=1, keepdims=True) + 1e-06)
    return (wide_rows * inverse * ffn_gain[None, :]).astype(jnp.bfloat16)


def per_device(
    stream_in,
    queries,
    key_proj,
    values,
    attn_gate,
    decay_rates,
    attn_gain,
    out_weight,
    ffn_gain,
    routing,
    route_weights,
    w_gate,
    w_up,
    w_down,
):
    rows_here, model_width = stream_in.shape
    head_count = decay_rates.shape[0]
    head_size = queries.shape[1] // head_count
    exp_count = lax.axis_size("exp")
    own_index = lax.axis_index("exp")
    capacity = rows_here // 16
    own_rows = rows_here // exp_count
    per_block = own_rows + capacity
    query_heads = queries.reshape(rows_here, head_count, head_size)
    key_heads = key_proj.reshape(rows_here, head_count, head_size)
    value_heads = values.reshape(rows_here, head_count, head_size)
    positions = jnp.arange(rows_here, dtype=jnp.float32)
    tail_decay = jnp.exp(-decay_rates[None, :] * (rows_here - 1.0 - positions)[:, None])
    weighted_keys = key_heads.astype(jnp.float32) * tail_decay[:, :, None]
    local_state = jnp.einsum(
        "jhd,jhe->hde", weighted_keys, value_heads.astype(jnp.float32), precision=HIGHEST
    )
    prior_state = decayed_prefix(local_state, decay_rates, rows_here)
    scores = jnp.einsum("ihd,jhd->hij", query_heads, key_heads, preferred_element_type=jnp.float32)
    distance = positions[:, None] - positions[None, :]
    decay_mask = jnp.where(
        distance[None] >= 0.0,
        jnp.exp(-decay_rates[:, None, None] * jnp.maximum(distance, 0.0)[None]),
        0.0,
    )
    near_weights = (scores * decay_mask).astype(jnp.bfloat16)
    near_part = jnp.einsum(
        "hij,jhd->ihd", near_weights, value_heads, preferred_element_type=jnp.float32
    )
    lead_decay = jnp.exp(-decay_rates[None, :] * (positions + 1.0)[:, None])
    far_part = jnp.einsum(
        "ihd,hde->ihe",
        query_heads.astype(jnp.float32) * lead_decay[:, :, None],
        prior_state,
        precision=HIGHEST,
    )
    attended = near_part + far_part
    inverse = lax.rsqrt(jnp.mean(attended * attended, axis=2, keepdims=True) + 1e-06)
    normed = (attended * inverse).reshape(rows_here, head_count * head_size)
    mixed_heads = (
        normed * attn_gain[None, :] * jax.nn.sigmoid(attn_gate.astype(jnp.float32))
    ).astype(jnp.bfloat16)
    held_ids = jnp.arange(exp_count, dtype=jnp.int32)
    hit_mask = routing[:, :, None] == held_ids[None, None, :]
    member = jnp.sum(hit_mask.astype(jnp.int32), axis=1)
    gate_of = jnp.sum(jnp.where(hit_mask, route_weights[:, :, None], 0.0), axis=1)
    slot_rank = jnp.cumsum(member, axis=0) - 1
    slot_index = jnp.arange(capacity, dtype=jnp.int32)
    pick_mask = (member[:, :, None] == 1) & (slot_rank[:, :, None] == slot_index[None, None, :])
    selector = pick_mask.reshape(rows_here, exp_count * capacity).T.astype(jnp.bfloat16)
    slot_weight = jnp.sum(jnp.where(pick_mask, gate_of[:, :, None], 0.0), axis=0)
    slot_mixed = jnp.dot(selector, mixed_heads, preferred_element_type=jnp.float32).astype(
        jnp.bfloat16
    )
    row_blocks = jnp.concatenate(
        [mixed_heads.reshape(exp_count, own_rows, -1), slot_mixed.reshape(exp_count, capacity, -1)],
        axis=1,
    )
    stacked = row_blocks.reshape(exp_count * per_block, head_count * head_size)
    pair_rows = lax.all_gather(stacked, "core", axis=0, tiled=True)
    half_weight = lax.all_gather(out_weight, "yz", axis=1, tiled=True)
    half_width = half_weight.shape[1]
    partial_rows = jnp.dot(pair_rows, half_weight, preferred_element_type=jnp.float32)
    partial_term = partial_rows.astype(jnp.bfloat16).reshape(2, exp_count, per_block, half_width)
    swapped = lax.all_to_all(partial_term, "exp", 1, 1, tiled=True)
    head_sum = jnp.sum(swapped.astype(jnp.float32), axis=1)
    by_parity = lax.all_to_all(head_sum, "core", 0, 0, tiled=True)
    block_width = out_weight.shape[1]
    projected = (
        by_parity.reshape(2, per_block, half_width // block_width, block_width)
        .transpose(1, 2, 0, 3)
        .reshape(per_block, model_width)
    )
    stream_own = lax.dynamic_slice_in_dim(stream_in, own_index * own_rows, own_rows, 0)
    own_selector = lax.dynamic_slice_in_dim(selector, own_index * capacity, capacity, 0)
    stream_slots = jnp.dot(own_selector, stream_in, preferred_element_type=jnp.float32)
    residual_rows = jnp.concatenate([stream_own.astype(jnp.float32), stream_slots], axis=0)
    hidden_rows = (residual_rows + projected).astype(jnp.bfloat16)
    residual_out = hidden_rows[:own_rows]
    slot_hidden = hidden_rows[own_rows:]
    outgoing = normalize_rows(slot_hidden, ffn_gain)
    ctx_count = lax.axis_size(CTX)
    row_piece = lax.all_gather(outgoing, CTX, axis=0, tiled=True)
    gate_part = jnp.dot(row_piece, w_gate[0], preferred_element_type=jnp.float32)
    up_part = jnp.dot(row_piece, w_up[0], preferred_element_type=jnp.float32)
    activated = (jax.nn.silu(gate_part) * up_part).astype(jnp.bfloat16)
    down_part = jnp.dot(activated, w_down[0], preferred_element_type=jnp.float32)
    down_blocks = lax.all_to_all(
        down_part.astype(jnp.bfloat16).reshape(ctx_count, capacity, model_width),
        CTX,
        0,
        0,
        tiled=True,
    )
    summed_down = jnp.sum(down_blocks.astype(jnp.float32), axis=0)
    own_weight = lax.dynamic_index_in_dim(slot_weight, own_index, 0, keepdims=False)
    expert_out = (
        (summed_down * own_weight[:, None])
        .astype(jnp.bfloat16)
        .reshape(1, 1, capacity, model_width)
    )
    return (residual_out, expert_out)


def solution(mesh):
    ctx_size, exp_size = mesh.devices.shape
    split = jax.sharding.Mesh(
        mesh.devices.reshape(ctx_size // 2, 2, exp_size), ("yz", "core", "exp")
    )
    return jax.shard_map(
        per_device,
        mesh=split,
        in_specs=(
            P(CTX, None),
            P(CTX, "exp"),
            P(CTX, "exp"),
            P(CTX, "exp"),
            P(CTX, "exp"),
            P("exp"),
            P("exp"),
            P("exp", CTX),
            P(),
            P(CTX, None),
            P(CTX, None),
            P("exp", None, CTX),
            P("exp", None, CTX),
            P("exp", CTX, None),
        ),
        out_specs=(P((CTX[0], CTX[1], "exp"), None), P(CTX, "exp", None, None)),
        check_vma=False,
    )
```

profile of v0, /device:TPU:1, one launch (start us, length us, event | category | flops | bytes accessed | tf_op | source)
XLA Modules:
  0.0 395.3 jit_solution(3186503120921249758)
XLA Ops:
  14.0 4.9 %collective-permute-start = (bf16[16,128,128]{2,1,0:T(8,128)(2,1)S(1)}, bf16[16,128,128]{2,1,0:T(8,128)(2,1)S(1)}, u32[]{:S(2)}, u32[]{:S(2)}) collective-permute-start(bf16[16,128,128]{2,1,0:T(8,128)(2,1)S(1)} %convolution_convert_fusion.3), channel_id=1, source_target_pairs={{0,4},{4,8},{8,12},{12,16},{16,20},{20,24},{24,28},{28,32},{32,36}... | collective-permute-start | bytes 1572872 | tf_op jit(solution)/shard_map/ppermute | solution.py:15
  18.9 6.1 %collective-permute-done = bf16[16,128,128]{2,1,0:T(8,128)(2,1)S(1)} collective-permute-done((bf16[16,128,128]{2,1,0:T(8,128)(2,1)S(1)}, bf16[16,128,128]{2,1,0:T(8,128)(2,1)S(1)}, u32[]{:S(2)}, u32[]{:S(2)}) %collective-permute-start) | collective-permute-done | bytes 524320 | tf_op jit(solution)/shard_map/ppermute | solution.py:15
  25.0 4.4 %collective-permute-start.1 = (bf16[16,128,128]{2,1,0:T(8,128)(2,1)S(1)}, bf16[16,128,128]{2,1,0:T(8,128)(2,1)S(1)}, u32[]{:S(2)}, u32[]{:S(2)}) collective-permute-start(bf16[16,128,128]{2,1,0:T(8,128)(2,1)S(1)} %collective-permute-done), channel_id=1, source_target_pairs={{0,4},{4,8},{8,12},{12,16},{16,20},{20,24},{24,28},{28,32},{32,36}... | collective-permute-start | bytes 1572872 | tf_op jit(solution)/shard_map/ppermute | solution.py:15
  29.4 6.1 %collective-permute-done.1 = bf16[16,128,128]{2,1,0:T(8,128)(2,1)S(1)} collective-permute-done((bf16[16,128,128]{2,1,0:T(8,128)(2,1)S(1)}, bf16[16,128,128]{2,1,0:T(8,128)(2,1)S(1)}, u32[]{:S(2)}, u32[]{:S(2)}) %collective-permute-start.1) | collective-permute-done | bytes 524320 | tf_op jit(solution)/shard_map/ppermute | solution.py:15
  35.8 3.6 collective-permute-start.2
  39.4 10.2 %collective-permute-done.2 = bf16[16,128,128]{2,1,0:T(8,128)(2,1)S(1)} collective-permute-done((bf16[16,128,128]{2,1,0:T(8,128)(2,1)S(1)}, bf16[16,128,128]{2,1,0:T(8,128)(2,1)S(1)}, u32[]{:S(2)}, u32[]{:S(2)}) %collective-permute-start.2) | collective-permute-done | bytes 524320 | tf_op jit(solution)/shard_map/ppermute | solution.py:15
  50.0 6.1 %collective-permute-start.3 = (bf16[16,128,128]{2,1,0:T(8,128)(2,1)S(1)}, bf16[16,128,128]{2,1,0:T(8,128)(2,1)S(1)}, u32[]{:S(2)}, u32[]{:S(2)}) collective-permute-start(bf16[16,128,128]{2,1,0:T(8,128)(2,1)S(1)} %fusion.69), channel_id=1, source_target_pairs={{0,16},{4,20},{8,24},{12,28},{16,32},{20,36},{24,40},{28,44},{32,4... | collective-permute-start | bytes 1572872 | tf_op jit(solution)/shard_map/ppermute | solution.py:15
  56.1 9.6 %collective-permute-done.3 = bf16[16,128,128]{2,1,0:T(8,128)(2,1)S(1)} collective-permute-done((bf16[16,128,128]{2,1,0:T(8,128)(2,1)S(1)}, bf16[16,128,128]{2,1,0:T(8,128)(2,1)S(1)}, u32[]{:S(2)}, u32[]{:S(2)}) %collective-permute-start.3) | collective-permute-done | bytes 524320 | tf_op jit(solution)/shard_map/ppermute | solution.py:15
  67.0 4.0 %collective-permute-start.4 = (bf16[16,128,128]{2,1,0:T(8,128)(2,1)}, bf16[16,128,128]{2,1,0:T(8,128)(2,1)}, u32[]{:S(2)}, u32[]{:S(2)}) collective-permute-start(bf16[16,128,128]{2,1,0:T(8,128)(2,1)} %fusion.27), channel_id=1, source_target_pairs={{0,32},{4,36},{8,40},{12,44},{16,48},{20,52},{24,56},{28,60},{32,6... | collective-permute-start | bytes 1572872 | tf_op jit(solution)/shard_map/ppermute | solution.py:15
  81.7 4.1 %collective-permute-start.5 = (bf16[16,128,128]{2,1,0:T(8,128)(2,1)}, bf16[16,128,128]{2,1,0:T(8,128)(2,1)}, u32[]{:S(2)}, u32[]{:S(2)}) collective-permute-start(bf16[16,128,128]{2,1,0:T(8,128)(2,1)} %fusion.68), channel_id=1, source_target_pairs={{0,64},{4,68},{8,72},{12,76},{16,80},{20,84},{24,88},{28,92},{32,9... | collective-permute-start | bytes 1572872 | tf_op jit(solution)/shard_map/ppermute | solution.py:15
  92.9 5.1 %multiply_reduce_fusion = (f32[128,16]{0,1:T(8,128)S(1)}, f32[128,16,128]{0,2,1:T(8,128)S(1)}) fusion(f32[128,16,128]{0,2,1:T(8,128)} %convolution_bitcast_fusion.1, f32[128,16]{0,1:T(8,128)S(1)} %get-tuple-element.8, bf16[16,128,128]{2,1,0:T(8,128)(2,1)} %collective-permute-done.5, f32[16]{0:T(128)} %get-tuple-element.2, ...), kind=kOutput, calls=%fused_computation.21 | convolution fusion | flops 408156160 | bytes 5783872 | tf_op jit(solution)/shard_map/ihd,hde->ihe/dot_general | solution.py:78
  105.9 22.1 %all-gather.4.cloned.1.call-done = bf16[320,2048]{1,0:T(8,128)(2,1)} async-done(((bf16[160,2048]{1,0:T(8,128)(2,1)}), bf16[320,2048]{1,0:T(8,128)(2,1)}) %all-gather.4.cloned.1.call-update) | async-done | bytes 1310736 | tf_op jit(solution)/shard_map/all_gather | solution.py:107
  128.0 93.3 %all-gather.6.cloned.1.call-done = bf16[2048,3072]{0,1:T(8,128)(2,1)} async-done(((bf16[2048,192]{0,1:T(8,128)(2,1)}), bf16[2048,3072]{0,1:T(8,128)(2,1)}) %all-gather.6.cloned.1.call-update) | async-done | bytes 12582928 | tf_op jit(solution)/shard_map/all_gather | solution.py:108
  221.2 9.2 %convolution_convert_fusion.1 = bf16[320,3072]{1,0:T(8,128)(2,1)S(1)} fusion(bf16[320,2048]{1,0:T(8,128)(2,1)} %all-gather.4.cloned.1.call-done, bf16[2048,3072]{0,1:T(8,128)(2,1)} %all-gather.6.cloned.1.call-done), kind=kOutput, calls=%fused_computation.3 | convolution fusion | flops 4027514880 | bytes 15859712 | tf_op jit(solution)/shard_map/dot_general | solution.py:110
  231.9 4.4 %all-to-all-start = ((bf16[2,4,40,3072]{3,2,0,1:T(8,128)(2,1)}), bf16[2,4,40,3072]{3,2,0,1:T(8,128)(2,1)}, u32[]{:S(2)}, u32[]{:S(2)}) async-start(bf16[2,4,40,3072]{3,2,0,1:T(8,128)(2,1)} %copy.71), calls=%async_computation | async-start | bytes 3932160 | tf_op jit(solution)/shard_map/all_to_all | solution.py:112
  240.8 19.9 %all-to-all-done = bf16[2,4,40,3072]{3,2,0,1:T(8,128)(2,1)} async-done(((bf16[2,4,40,3072]{3,2,0,1:T(8,128)(2,1)}), bf16[2,4,40,3072]{3,2,0,1:T(8,128)(2,1)}, u32[]{:S(2)}, u32[]{:S(2)}) %all-to-all-start) | async-done | bytes 1966112 | tf_op jit(solution)/shard_map/all_to_all | solution.py:112
  262.7 6.6 %all_to_all.15 = f32[2,40,3072]{2,1,0:T(8,128)} all-to-all(f32[2,40,3072]{2,1,0:T(8,128)S(1)} %convert_reduce_fusion.1), channel_id=1, replica_groups=mesh['yz'=16,'core'=2,'exp'=4] {'core'}, dimensions={0} | all-to-all | bytes 1966080 | tf_op jit(solution)/shard_map/all_to_all | solution.py:114
  272.2 3.5 copy.72
  275.7 3.6 reshape.211
  283.2 43.2 %all-gather.8.cloned.1.call-done = bf16[256,6144]{1,0:T(8,128)(2,1)} async-done(((bf16[8,6144]{1,0:T(8,128)(2,1)}), bf16[256,6144]{1,0:T(8,128)(2,1)}) %all-gather.8.cloned.1.call-update) | async-done | bytes 3145744 | tf_op jit(solution)/shard_map/all_gather | solution.py:130
  326.3 4.8 %fusion.4 = f32[256,288]{0,1:T(8,128)} fusion(bf16[256,6144]{1,0:T(8,128)(2,1)} %all-gather.8.cloned.1.call-done, bf16[1,6144,288]{1,2,0:T(8,128)(2,1)} %param.25), kind=kOutput, calls=%fused_computation.8 | convolution fusion | flops 905969664 | bytes 6979584 | tf_op jit(solution)/shard_map/dot_general | solution.py:131
  331.1 9.4 %fusion = bf16[32,8,6144]{2,1,0:T(8,128)(2,1)} fusion(bf16[1,288,6144]{2,1,0:T(8,128)(2,1)S(1)} %copy-done, bf16[256,6144]{1,0:T(8,128)(2,1)} %all-gather.8.cloned.1.call-done, bf16[1,6144,288]{1,2,0:T(8,128)(2,1)} %param.26, f32[256,288]{0,1:T(8,128)} %fusion.4), kind=kOutput, calls=%fused_computation.1 | convolution fusion | flops 1813954560 | bytes 13664256 | tf_op jit(solution)/shard_map/dot_general | solution.py:134
  340.5 5.4 %all-to-all-start.2 = ((bf16[32,8,6144]{2,1,0:T(8,128)(2,1)}), bf16[32,8,6144]{2,1,0:T(8,128)(2,1)}, u32[]{:S(2)}, u32[]{:S(2)}) async-start(bf16[32,8,6144]{2,1,0:T(8,128)(2,1)} %fusion), calls=%async_computation.2 | async-start | bytes 6291456 | tf_op jit(solution)/shard_map/all_to_all | solution.py:135
  347.8 37.9 %all-to-all-done.2 = bf16[32,8,6144]{2,1,0:T(8,128)(2,1)} async-done(((bf16[32,8,6144]{2,1,0:T(8,128)(2,1)}), bf16[32,8,6144]{2,1,0:T(8,128)(2,1)}, u32[]{:S(2)}, u32[]{:S(2)}) %all-to-all-start.2) | async-done | bytes 3145760 | tf_op jit(solution)/shard_map/all_to_all | solution.py:135
  (80 shorter events, 53.9 us)
Async XLA Ops:
  7.2 324.0 %copy-start = (bf16[1,288,6144]{2,1,0:T(8,128)(2,1)S(1)}, bf16[1,288,6144]{2,1,0:T(8,128)(2,1)}, u32[]{:S(2)}) copy-start(bf16[1,288,6144]{2,1,0:T(8,128)(2,1)} %param.27) | copy-start | bytes 10616836
  7.2 120.8 %all-gather.4.cloned.1.call-start = ((), (), s32[]{:S(2)}) async-start(), calls=%async_computation.3 | async-start | bytes 1966080 | tf_op jit(solution)/shard_map/all_gather | solution.py:107
  9.3 56.5 %copy-start.7 = (f32[16]{0:T(128)}, f32[16]{0:T(128)S(1)}, u32[]{:S(2)}) copy-start(f32[16]{0:T(128)S(1)} %get-tuple-element.4) | copy-start | bytes 196
  9.3 69.3 %copy-start.6 = (f32[16]{0:T(128)}, f32[16]{0:T(128)S(1)}, u32[]{:S(2)}) copy-start(f32[16]{0:T(128)S(1)} %get-tuple-element.3) | copy-start | bytes 196
  11.3 54.4 %copy-start.10 = (f32[16]{0:T(128)S(1)}, f32[16]{0:T(128)}, u32[]{:S(2)}) copy-start(f32[16]{0:T(128)} %get-tuple-element.5) | copy-start | bytes 196
  14.0 11.0 %collective-permute-start = (bf16[16,128,128]{2,1,0:T(8,128)(2,1)S(1)}, bf16[16,128,128]{2,1,0:T(8,128)(2,1)S(1)}, u32[]{:S(2)}, u32[]{:S(2)}) collective-permute-start(bf16[16,128,128]{2,1,0:T(8,128)(2,1)S(1)} %convolution_convert_fusion.3), channel_id=1, source_target_pairs={{0,4},{4,8},{8,12},{12,16},{16,20},{20,24},{24,28},{28,32},{32,36}... | collective-permute-start | bytes 1572872 | tf_op jit(solution)/shard_map/ppermute | solution.py:15
  25.0 42.0 %copy-start.1 = (bf16[16,128,128]{2,1,0:T(8,128)(2,1)}, bf16[16,128,128]{2,1,0:T(8,128)(2,1)S(1)}, u32[]{:S(2)}) copy-start(bf16[16,128,128]{2,1,0:T(8,128)(2,1)S(1)} %collective-permute-done) | copy-start | bytes 1572868
  25.0 10.5 %collective-permute-start.1 = (bf16[16,128,128]{2,1,0:T(8,128)(2,1)S(1)}, bf16[16,128,128]{2,1,0:T(8,128)(2,1)S(1)}, u32[]{:S(2)}, u32[]{:S(2)}) collective-permute-start(bf16[16,128,128]{2,1,0:T(8,128)(2,1)S(1)} %collective-permute-done), channel_id=1, source_target_pairs={{0,4},{4,8},{8,12},{12,16},{16,20},{20,24},{24,28},{28,32},{32,36}... | collective-permute-start | bytes 1572872 | tf_op jit(solution)/shard_map/ppermute | solution.py:15
  35.5 31.5 %copy-start.2 = (bf16[16,128,128]{2,1,0:T(8,128)(2,1)}, bf16[16,128,128]{2,1,0:T(8,128)(2,1)S(1)}, u32[]{:S(2)}) copy-start(bf16[16,128,128]{2,1,0:T(8,128)(2,1)S(1)} %collective-permute-done.1) | copy-start | bytes 1572868
  35.5 35.5 %copy-start.12 = (s32[128,2]{0,1:T(2,128)S(1)}, s32[128,2]{0,1:T(2,128)}, u32[]{:S(2)}) copy-start(s32[128,2]{0,1:T(2,128)} %param.23) | copy-start | bytes 3076
  35.8 13.8 %collective-permute-start.2 = (bf16[16,128,128]{2,1,0:T(8,128)(2,1)S(1)}, bf16[16,128,128]{2,1,0:T(8,128)(2,1)S(1)}, u32[]{:S(2)}, u32[]{:S(2)}) collective-permute-start(bf16[16,128,128]{2,1,0:T(8,128)(2,1)S(1)} %fusion.26), channel_id=1, source_target_pairs={{0,8},{4,12},{8,16},{12,20},{16,24},{20,28},{24,32},{28,36},{32,40... | collective-permute-start | bytes 1572872 | tf_op jit(solution)/shard_map/ppermute | solution.py:15
  49.6 21.5 %copy-start.3 = (bf16[16,128,128]{2,1,0:T(8,128)(2,1)}, bf16[16,128,128]{2,1,0:T(8,128)(2,1)S(1)}, u32[]{:S(2)}) copy-start(bf16[16,128,128]{2,1,0:T(8,128)(2,1)S(1)} %collective-permute-done.2) | copy-start | bytes 1572868
  50.0 15.7 %collective-permute-start.3 = (bf16[16,128,128]{2,1,0:T(8,128)(2,1)S(1)}, bf16[16,128,128]{2,1,0:T(8,128)(2,1)S(1)}, u32[]{:S(2)}, u32[]{:S(2)}) collective-permute-start(bf16[16,128,128]{2,1,0:T(8,128)(2,1)S(1)} %fusion.69), channel_id=1, source_target_pairs={{0,16},{4,20},{8,24},{12,28},{16,32},{20,36},{24,40},{28,44},{32,4... | collective-permute-start | bytes 1572872 | tf_op jit(solution)/shard_map/ppermute | solution.py:15
  65.7 5.3 %copy-start.4 = (bf16[16,128,128]{2,1,0:T(8,128)(2,1)}, bf16[16,128,128]{2,1,0:T(8,128)(2,1)S(1)}, u32[]{:S(2)}) copy-start(bf16[16,128,128]{2,1,0:T(8,128)(2,1)S(1)} %collective-permute-done.3) | copy-start | bytes 1572868
  67.0 11.6 %collective-permute-start.4 = (bf16[16,128,128]{2,1,0:T(8,128)(2,1)}, bf16[16,128,128]{2,1,0:T(8,128)(2,1)}, u32[]{:S(2)}, u32[]{:S(2)}) collective-permute-start(bf16[16,128,128]{2,1,0:T(8,128)(2,1)} %fusion.27), channel_id=1, source_target_pairs={{0,32},{4,36},{8,40},{12,44},{16,48},{20,52},{24,56},{28,60},{32,6... | collective-permute-start | bytes 1572872 | tf_op jit(solution)/shard_map/ppermute | solution.py:15
  81.7 11.2 %collective-permute-start.5 = (bf16[16,128,128]{2,1,0:T(8,128)(2,1)}, bf16[16,128,128]{2,1,0:T(8,128)(2,1)}, u32[]{:S(2)}, u32[]{:S(2)}) collective-permute-start(bf16[16,128,128]{2,1,0:T(8,128)(2,1)} %fusion.68), channel_id=1, source_target_pairs={{0,64},{4,68},{8,72},{12,76},{16,80},{20,84},{24,88},{28,92},{32,9... | collective-permute-start | bytes 1572872 | tf_op jit(solution)/shard_map/ppermute | solution.py:15
  98.0 5.3 %copy-start.9 = (pred[128,4]{0,1:T(4,128)(4,1)S(1)}, pred[128,4]{0,1:T(4,128)(4,1)}, u32[]{:S(2)}) copy-start(pred[128,4]{0,1:T(4,128)(4,1)} %broadcast_compare_fusion) | copy-start | bytes 1540
  105.1 116.1 %all-gather.6.cloned.1.call-start = ((), (), s32[]{:S(2)}) async-start(), calls=%async_computation.4 | async-start | bytes 13369344 | tf_op jit(solution)/shard_map/all_gather | solution.py:108
  230.5 5.9 %copy-start.11 = (s32[32]{0:T(128)S(1)}, s32[32]{0:T(128)}, u32[]{:S(2)}) copy-start(s32[32]{0:T(128)} %eq.56) | copy-start | bytes 388
  231.9 28.8 %all-to-all-start = ((bf16[2,4,40,3072]{3,2,0,1:T(8,128)(2,1)}), bf16[2,4,40,3072]{3,2,0,1:T(8,128)(2,1)}, u32[]{:S(2)}, u32[]{:S(2)}) async-start(bf16[2,4,40,3072]{3,2,0,1:T(8,128)(2,1)} %copy.71), calls=%async_computation | async-start | bytes 3932160 | tf_op jit(solution)/shard_map/all_to_all | solution.py:112
  236.3 90.0 %all-gather.8.cloned.1.call-start = ((), (), s32[]{:S(2)}) async-start(), calls=%async_computation.5 | async-start | bytes 3244032 | tf_op jit(solution)/shard_map/all_gather | solution.py:130
  340.5 5.5 %copy-start.13 = (s32[128,2]{0,1:T(2,128)S(1)}, s32[128,2]{0,1:T(2,128)}, u32[]{:S(2)}) copy-start(s32[128,2]{0,1:T(2,128)} %param.23) | copy-start | bytes 3076
  340.5 5.5 %copy-start.14 = (f32[128,2]{0,1:T(2,128)S(1)}, f32[128,2]{0,1:T(2,128)}, u32[]{:S(2)}) copy-start(f32[128,2]{0,1:T(2,128)} %param.24) | copy-start | bytes 3076
  340.5 45.3 %all-to-all-start.2 = ((bf16[32,8,6144]{2,1,0:T(8,128)(2,1)}), bf16[32,8,6144]{2,1,0:T(8,128)(2,1)}, u32[]{:S(2)}, u32[]{:S(2)}) async-start(bf16[32,8,6144]{2,1,0:T(8,128)(2,1)} %fusion), calls=%async_computation.2 | async-start | bytes 6291456 | tf_op jit(solution)/shard_map/all_to_all | solution.py:135
  (2 other events, 4.5 us)
Sparse Core Ops, SparseCore 0:
  105.2 22.6 all-gather.3
  130.1 91.0 all-gather.5
  283.3 42.9 all-gather.7
where the time goes:
time: 397 us; the launch traced here: 395 us
  waiting for transfers between devices  252 us (63%)
  starting transfers between devices  37.3 us (9%)
  matrix products  36.7 us (9%)
  other arithmetic  26.8 us (7%)
  local copies, waits for them, and re-layouts  22 us (6%)
  between operations  14 us (4%)
  blocking collectives  6.59 us (2%)
    all_gather x1, waiting for transfers between devices, per_device(): half_weight = lax.all_gather(out_weight, 'yz', axis=1, tiled=True)  93.3 us
    all_gather x1, waiting for transfers between devices, per_device(): row_piece = lax.all_gather(outgoing, CTX, axis=0, tiled=True)  43.2 us
    all_to_all x1, waiting for transfers between devices, per_device(): lax.all_to_all(down_part.astype(jnp.bfloat16).reshape(ctx_count, capacity...  37.9 us
    ppermute x6, waiting for transfers between devices, shift(): lax.ppermute(value.astype(jnp.bfloat16), CTX, pairs).astype(jnp.float32)  35.1 us
    ppermute x6, starting transfers between devices, shift(): lax.ppermute(value.astype(jnp.bfloat16), CTX, pairs).astype(jnp.float32)  27.1 us
    all_gather x1, waiting for transfers between devices, per_device(): pair_rows = lax.all_gather(stacked, 'core', axis=0, tiled=True)  22.1 us
    all_to_all x1, waiting for transfers between devices, per_device(): swapped = lax.all_to_all(partial_term, 'exp', 1, 1, tiled=True)  19.9 us
    dot_general x1, matrix products, per_device(): jnp.dot(activated, w_down[0], preferred_element_type=jnp.float32)  9.36 us
  transfers between devices with their start and end apart: 11, of which 10 were waited for; matrix products, arithmetic and copies ran while one was open for 5% of the time, Pallas kernels for 0%

commit v1 on v0

--- a/solution.py
+++ b/solution.py
@@ -109,7 +109,12 @@
     half_width = half_weight.shape[1]
     partial_rows = jnp.dot(pair_rows, half_weight, preferred_element_type=jnp.float32)
     partial_term = partial_rows.astype(jnp.bfloat16).reshape(2, exp_count, per_block, half_width)
-    swapped = lax.all_to_all(partial_term, "exp", 1, 1, tiled=True)
+    swapped = jnp.concatenate(
+        lax.all_to_all(
+            jnp.stack(jnp.split(partial_term, lax.axis_size("exp"), axis=1)), "exp", 0, 0
+        ),
+        axis=1,
+    )
     head_sum = jnp.sum(swapped.astype(jnp.float32), axis=1)
     by_parity = lax.all_to_all(head_sum, "core", 0, 0, tiled=True)
     block_width = out_weight.shape[1]

time: 397 us -> 397 us (level)
  transfers between devices with their start and end apart: 11 -> 11, of which waited for: 10 -> 10; matrix products, arithmetic and copies ran while one was open for 5% -> 4% of each run, Pallas kernels for 0% -> 0%
where the time goes in v1:
time: 397 us; the launch traced here: 396 us
  waiting for transfers between devices  252 us (63%)
  starting transfers between devices  37.2 us (9%)
  matrix products  36.7 us (9%)
  other arithmetic  28.3 us (7%)
  local copies, waits for them, and re-layouts  20.7 us (5%)
  between operations  14 us (4%)
  blocking collectives  6.6 us (2%)
    all_gather x1, waiting for transfers between devices, per_device(): half_weight = lax.all_gather(out_weight, 'yz', axis=1, tiled=True)  93.3 us
    all_gather x1, waiting for transfers between devices, per_device(): row_piece = lax.all_gather(outgoing, CTX, axis=0, tiled=True)  43.2 us
    all_to_all x1, waiting for transfers between devices, per_device(): lax.all_to_all(down_part.astype(jnp.bfloat16).reshape(ctx_count, capacity...  37.9 us
    ppermute x6, waiting for transfers between devices, shift(): lax.ppermute(value.astype(jnp.bfloat16), CTX, pairs).astype(jnp.float32)  35.1 us
    ppermute x6, starting transfers between devices, shift(): lax.ppermute(value.astype(jnp.bfloat16), CTX, pairs).astype(jnp.float32)  27.1 us
    all_gather x1, waiting for transfers between devices, per_device(): pair_rows = lax.all_gather(stacked, 'core', axis=0, tiled=True)  22.1 us
    all_to_all x1, waiting for transfers between devices, per_device(): lax.all_to_all(jnp.stack(jnp.split(partial_term, lax.axis_size('exp'), ax...  19.9 us
    dot_general x1, matrix products, per_device(): jnp.dot(activated, w_down[0], preferred_element_type=jnp.float32)  9.37 us
  transfers between devices with their start and end apart: 11, of which 10 were waited for; matrix products, arithmetic and copies ran while one was open for 4% of the time, Pallas kernels for 0%

profile of v1, /device:TPU:1, one launch (start us, length us, event | category | flops | bytes accessed | tf_op | source)
XLA Modules:
  0.0 395.6 jit_solution(17062926749366474211)
XLA Ops:
  14.0 4.9 %collective-permute-start = (bf16[16,128,128]{2,1,0:T(8,128)(2,1)S(1)}, bf16[16,128,128]{2,1,0:T(8,128)(2,1)S(1)}, u32[]{:S(2)}, u32[]{:S(2)}) collective-permute-start(bf16[16,128,128]{2,1,0:T(8,128)(2,1)S(1)} %convolution_convert_fusion.3), channel_id=1, source_target_pairs={{0,4},{4,8},{8,12},{12,16},{16,20},{20,24},{24,28},{28,32},{32,36}... | collective-permute-start | bytes 1572872 | tf_op jit(solution)/shard_map/ppermute | solution.py:15
  18.9 6.1 %collective-permute-done = bf16[16,128,128]{2,1,0:T(8,128)(2,1)S(1)} collective-permute-done((bf16[16,128,128]{2,1,0:T(8,128)(2,1)S(1)}, bf16[16,128,128]{2,1,0:T(8,128)(2,1)S(1)}, u32[]{:S(2)}, u32[]{:S(2)}) %collective-permute-start) | collective-permute-done | bytes 524320 | tf_op jit(solution)/shard_map/ppermute | solution.py:15
  25.0 4.4 %collective-permute-start.1 = (bf16[16,128,128]{2,1,0:T(8,128)(2,1)S(1)}, bf16[16,128,128]{2,1,0:T(8,128)(2,1)S(1)}, u32[]{:S(2)}, u32[]{:S(2)}) collective-permute-start(bf16[16,128,128]{2,1,0:T(8,128)(2,1)S(1)} %collective-permute-done), channel_id=1, source_target_pairs={{0,4},{4,8},{8,12},{12,16},{16,20},{20,24},{24,28},{28,32},{32,36}... | collective-permute-start | bytes 1572872 | tf_op jit(solution)/shard_map/ppermute | solution.py:15
  29.4 6.1 %collective-permute-done.1 = bf16[16,128,128]{2,1,0:T(8,128)(2,1)S(1)} collective-permute-done((bf16[16,128,128]{2,1,0:T(8,128)(2,1)S(1)}, bf16[16,128,128]{2,1,0:T(8,128)(2,1)S(1)}, u32[]{:S(2)}, u32[]{:S(2)}) %collective-permute-start.1) | collective-permute-done | bytes 524320 | tf_op jit(solution)/shard_map/ppermute | solution.py:15
  35.8 3.6 collective-permute-start.2
  39.4 10.2 %collective-permute-done.2 = bf16[16,128,128]{2,1,0:T(8,128)(2,1)S(1)} collective-permute-done((bf16[16,128,128]{2,1,0:T(8,128)(2,1)S(1)}, bf16[16,128,128]{2,1,0:T(8,128)(2,1)S(1)}, u32[]{:S(2)}, u32[]{:S(2)}) %collective-permute-start.2) | collective-permute-done | bytes 524320 | tf_op jit(solution)/shard_map/ppermute | solution.py:15
  50.0 6.1 %collective-permute-start.3 = (bf16[16,128,128]{2,1,0:T(8,128)(2,1)S(1)}, bf16[16,128,128]{2,1,0:T(8,128)(2,1)S(1)}, u32[]{:S(2)}, u32[]{:S(2)}) collective-permute-start(bf16[16,128,128]{2,1,0:T(8,128)(2,1)S(1)} %fusion.69), channel_id=1, source_target_pairs={{0,16},{4,20},{8,24},{12,28},{16,32},{20,36},{24,40},{28,44},{32,4... | collective-permute-start | bytes 1572872 | tf_op jit(solution)/shard_map/ppermute | solution.py:15
  56.1 9.6 %collective-permute-done.3 = bf16[16,128,128]{2,1,0:T(8,128)(2,1)S(1)} collective-permute-done((bf16[16,128,128]{2,1,0:T(8,128)(2,1)S(1)}, bf16[16,128,128]{2,1,0:T(8,128)(2,1)S(1)}, u32[]{:S(2)}, u32[]{:S(2)}) %collective-permute-start.3) | collective-permute-done | bytes 524320 | tf_op jit(solution)/shard_map/ppermute | solution.py:15
  67.0 4.0 %collective-permute-start.4 = (bf16[16,128,128]{2,1,0:T(8,128)(2,1)}, bf16[16,128,128]{2,1,0:T(8,128)(2,1)}, u32[]{:S(2)}, u32[]{:S(2)}) collective-permute-start(bf16[16,128,128]{2,1,0:T(8,128)(2,1)} %fusion.27), channel_id=1, source_target_pairs={{0,32},{4,36},{8,40},{12,44},{16,48},{20,52},{24,56},{28,60},{32,6... | collective-permute-start | bytes 1572872 | tf_op jit(solution)/shard_map/ppermute | solution.py:15
  81.7 4.1 %collective-permute-start.5 = (bf16[16,128,128]{2,1,0:T(8,128)(2,1)}, bf16[16,128,128]{2,1,0:T(8,128)(2,1)}, u32[]{:S(2)}, u32[]{:S(2)}) collective-permute-start(bf16[16,128,128]{2,1,0:T(8,128)(2,1)} %fusion.68), channel_id=1, source_target_pairs={{0,64},{4,68},{8,72},{12,76},{16,80},{20,84},{24,88},{28,92},{32,9... | collective-permute-start | bytes 1572872 | tf_op jit(solution)/shard_map/ppermute | solution.py:15
  92.8 5.1 %multiply_reduce_fusion = (f32[128,16]{0,1:T(8,128)S(1)}, f32[128,16,128]{0,2,1:T(8,128)S(1)}) fusion(f32[128,16,128]{0,2,1:T(8,128)} %convolution_bitcast_fusion.1, f32[128,16]{0,1:T(8,128)S(1)} %get-tuple-element.12, bf16[16,128,128]{2,1,0:T(8,128)(2,1)} %collective-permute-done.5, f32[16]{0:T(128)} %get-tuple-element.6, ...), kind=kOutput, calls=%fused_computation.22 | convolution fusion | flops 408156160 | bytes 5783872 | tf_op jit(solution)/shard_map/ihd,hde->ihe/dot_general | solution.py:78
  105.8 22.1 %all-gather.4.cloned.1.call-done = bf16[320,2048]{1,0:T(8,128)(2,1)} async-done(((bf16[160,2048]{1,0:T(8,128)(2,1)}), bf16[320,2048]{1,0:T(8,128)(2,1)}) %all-gather.4.cloned.1.call-update) | async-done | bytes 1310736 | tf_op jit(solution)/shard_map/all_gather | solution.py:107
  127.9 93.3 %all-gather.6.cloned.1.call-done = bf16[2048,3072]{0,1:T(8,128)(2,1)} async-done(((bf16[2048,192]{0,1:T(8,128)(2,1)}), bf16[2048,3072]{0,1:T(8,128)(2,1)}) %all-gather.6.cloned.1.call-update) | async-done | bytes 12582928 | tf_op jit(solution)/shard_map/all_gather | solution.py:108
  221.2 9.2 %convolution_convert_fusion.1 = bf16[320,3072]{1,0:T(8,128)(2,1)S(1)} fusion(bf16[320,2048]{1,0:T(8,128)(2,1)} %all-gather.4.cloned.1.call-done, bf16[2048,3072]{0,1:T(8,128)(2,1)} %all-gather.6.cloned.1.call-done), kind=kOutput, calls=%fused_computation.3 | convolution fusion | flops 4027514880 | bytes 15859712 | tf_op jit(solution)/shard_map/dot_general | solution.py:110
  232.1 4.4 %all-to-all-start = ((bf16[4,2,1,40,3072]{4,3,1,2,0:T(8,128)(2,1)}), bf16[4,2,1,40,3072]{4,3,1,2,0:T(8,128)(2,1)}, u32[]{:S(2)}, u32[]{:S(2)}) async-start(bf16[4,2,1,40,3072]{4,3,1,2,0:T(8,128)(2,1)} %pad_maximum_fusion), calls=%async_computation | async-start | bytes 3932160 | tf_op jit(solution)/shard_map/all_to_all | solution.py:113
  241.0 19.9 %all-to-all-done = bf16[4,2,1,40,3072]{4,3,1,2,0:T(8,128)(2,1)} async-done(((bf16[4,2,1,40,3072]{4,3,1,2,0:T(8,128)(2,1)}), bf16[4,2,1,40,3072]{4,3,1,2,0:T(8,128)(2,1)}, u32[]{:S(2)}, u32[]{:S(2)}) %all-to-all-start) | async-done | bytes 1966112 | tf_op jit(solution)/shard_map/all_to_all | solution.py:113
  262.9 6.6 %all_to_all.15 = f32[2,40,3072]{2,1,0:T(8,128)} all-to-all(f32[2,40,3072]{2,1,0:T(8,128)S(1)} %convert_reduce_fusion.1), channel_id=1, replica_groups=mesh['yz'=16,'core'=2,'exp'=4] {'core'}, dimensions={0} | all-to-all | bytes 1966080 | tf_op jit(solution)/shard_map/all_to_all | solution.py:119
  272.4 3.5 copy.69
  275.9 3.6 reshape.214
  283.4 43.2 %all-gather.8.cloned.1.call-done = bf16[256,6144]{1,0:T(8,128)(2,1)} async-done(((bf16[8,6144]{1,0:T(8,128)(2,1)}), bf16[256,6144]{1,0:T(8,128)(2,1)}) %all-gather.8.cloned.1.call-update) | async-done | bytes 3145744 | tf_op jit(solution)/shard_map/all_gather | solution.py:135
  326.5 4.8 %fusion.4 = f32[256,288]{0,1:T(8,128)} fusion(bf16[256,6144]{1,0:T(8,128)(2,1)} %all-gather.8.cloned.1.call-done, bf16[1,6144,288]{1,2,0:T(8,128)(2,1)} %param.25), kind=kOutput, calls=%fused_computation.8 | convolution fusion | flops 905969664 | bytes 6979584 | tf_op jit(solution)/shard_map/dot_general | solution.py:136
  331.3 9.4 %fusion = bf16[32,8,6144]{2,1,0:T(8,128)(2,1)} fusion(bf16[1,288,6144]{2,1,0:T(8,128)(2,1)S(1)} %copy-done, bf16[256,6144]{1,0:T(8,128)(2,1)} %all-gather.8.cloned.1.call-done, bf16[1,6144,288]{1,2,0:T(8,128)(2,1)} %param.26, f32[256,288]{0,1:T(8,128)} %fusion.4), kind=kOutput, calls=%fused_computation.1 | convolution fusion | flops 1813954560 | bytes 13664256 | tf_op jit(solution)/shard_map/dot_general | solution.py:139
  340.7 5.4 %all-to-all-start.2 = ((bf16[32,8,6144]{2,1,0:T(8,128)(2,1)}), bf16[32,8,6144]{2,1,0:T(8,128)(2,1)}, u32[]{:S(2)}, u32[]{:S(2)}) async-start(bf16[32,8,6144]{2,1,0:T(8,128)(2,1)} %fusion), calls=%async_computation.2 | async-start | bytes 6291456 | tf_op jit(solution)/shard_map/all_to_all | solution.py:140
  348.1 37.9 %all-to-all-done.2 = bf16[32,8,6144]{2,1,0:T(8,128)(2,1)} async-done(((bf16[32,8,6144]{2,1,0:T(8,128)(2,1)}), bf16[32,8,6144]{2,1,0:T(8,128)(2,1)}, u32[]{:S(2)}, u32[]{:S(2)}) %all-to-all-start.2) | async-done | bytes 3145760 | tf_op jit(solution)/shard_map/all_to_all | solution.py:140
  (81 shorter events, 54.1 us)
Async XLA Ops:
  7.2 324.2 %copy-start = (bf16[1,288,6144]{2,1,0:T(8,128)(2,1)S(1)}, bf16[1,288,6144]{2,1,0:T(8,128)(2,1)}, u32[]{:S(2)}) copy-start(bf16[1,288,6144]{2,1,0:T(8,128)(2,1)} %param.27) | copy-start | bytes 10616836
  7.2 120.8 %all-gather.4.cloned.1.call-start = ((), (), s32[]{:S(2)}) async-start(), calls=%async_computation.3 | async-start | bytes 1966080 | tf_op jit(solution)/shard_map/all_gather | solution.py:107
  9.3 56.4 %copy-start.7 = (f32[16]{0:T(128)}, f32[16]{0:T(128)S(1)}, u32[]{:S(2)}) copy-start(f32[16]{0:T(128)S(1)} %get-tuple-element.8) | copy-start | bytes 196
  9.3 69.3 %copy-start.6 = (f32[16]{0:T(128)}, f32[16]{0:T(128)S(1)}, u32[]{:S(2)}) copy-start(f32[16]{0:T(128)S(1)} %get-tuple-element.7) | copy-start | bytes 196
  11.3 54.4 %copy-start.10 = (f32[16]{0:T(128)S(1)}, f32[16]{0:T(128)}, u32[]{:S(2)}) copy-start(f32[16]{0:T(128)} %get-tuple-element.9) | copy-start | bytes 196
  14.0 11.0 %collective-permute-start = (bf16[16,128,128]{2,1,0:T(8,128)(2,1)S(1)}, bf16[16,128,128]{2,1,0:T(8,128)(2,1)S(1)}, u32[]{:S(2)}, u32[]{:S(2)}) collective-permute-start(bf16[16,128,128]{2,1,0:T(8,128)(2,1)S(1)} %convolution_convert_fusion.3), channel_id=1, source_target_pairs={{0,4},{4,8},{8,12},{12,16},{16,20},{20,24},{24,28},{28,32},{32,36}... | collective-permute-start | bytes 1572872 | tf_op jit(solution)/shard_map/ppermute | solution.py:15
  25.0 42.0 %copy-start.1 = (bf16[16,128,128]{2,1,0:T(8,128)(2,1)}, bf16[16,128,128]{2,1,0:T(8,128)(2,1)S(1)}, u32[]{:S(2)}) copy-start(bf16[16,128,128]{2,1,0:T(8,128)(2,1)S(1)} %collective-permute-done) | copy-start | bytes 1572868
  25.0 10.5 %collective-permute-start.1 = (bf16[16,128,128]{2,1,0:T(8,128)(2,1)S(1)}, bf16[16,128,128]{2,1,0:T(8,128)(2,1)S(1)}, u32[]{:S(2)}, u32[]{:S(2)}) collective-permute-start(bf16[16,128,128]{2,1,0:T(8,128)(2,1)S(1)} %collective-permute-done), channel_id=1, source_target_pairs={{0,4},{4,8},{8,12},{12,16},{16,20},{20,24},{24,28},{28,32},{32,36}... | collective-permute-start | bytes 1572872 | tf_op jit(solution)/shard_map/ppermute | solution.py:15
  35.5 31.5 %copy-start.2 = (bf16[16,128,128]{2,1,0:T(8,128)(2,1)}, bf16[16,128,128]{2,1,0:T(8,128)(2,1)S(1)}, u32[]{:S(2)}) copy-start(bf16[16,128,128]{2,1,0:T(8,128)(2,1)S(1)} %collective-permute-done.1) | copy-start | bytes 1572868
  35.5 35.5 %copy-start.12 = (s32[128,2]{0,1:T(2,128)S(1)}, s32[128,2]{0,1:T(2,128)}, u32[]{:S(2)}) copy-start(s32[128,2]{0,1:T(2,128)} %param.23) | copy-start | bytes 3076
  35.8 13.8 %collective-permute-start.2 = (bf16[16,128,128]{2,1,0:T(8,128)(2,1)S(1)}, bf16[16,128,128]{2,1,0:T(8,128)(2,1)S(1)}, u32[]{:S(2)}, u32[]{:S(2)}) collective-permute-start(bf16[16,128,128]{2,1,0:T(8,128)(2,1)S(1)} %fusion.26), channel_id=1, source_target_pairs={{0,8},{4,12},{8,16},{12,20},{16,24},{20,28},{24,32},{28,36},{32,40... | collective-permute-start | bytes 1572872 | tf_op jit(solution)/shard_map/ppermute | solution.py:15
  49.6 21.5 %copy-start.3 = (bf16[16,128,128]{2,1,0:T(8,128)(2,1)}, bf16[16,128,128]{2,1,0:T(8,128)(2,1)S(1)}, u32[]{:S(2)}) copy-start(bf16[16,128,128]{2,1,0:T(8,128)(2,1)S(1)} %collective-permute-done.2) | copy-start | bytes 1572868
  50.0 15.7 %collective-permute-start.3 = (bf16[16,128,128]{2,1,0:T(8,128)(2,1)S(1)}, bf16[16,128,128]{2,1,0:T(8,128)(2,1)S(1)}, u32[]{:S(2)}, u32[]{:S(2)}) collective-permute-start(bf16[16,128,128]{2,1,0:T(8,128)(2,1)S(1)} %fusion.69), channel_id=1, source_target_pairs={{0,16},{4,20},{8,24},{12,28},{16,32},{20,36},{24,40},{28,44},{32,4... | collective-permute-start | bytes 1572872 | tf_op jit(solution)/shard_map/ppermute | solution.py:15
  65.7 5.3 %copy-start.4 = (bf16[16,128,128]{2,1,0:T(8,128)(2,1)}, bf16[16,128,128]{2,1,0:T(8,128)(2,1)S(1)}, u32[]{:S(2)}) copy-start(bf16[16,128,128]{2,1,0:T(8,128)(2,1)S(1)} %collective-permute-done.3) | copy-start | bytes 1572868
  67.0 11.6 %collective-permute-start.4 = (bf16[16,128,128]{2,1,0:T(8,128)(2,1)}, bf16[16,128,128]{2,1,0:T(8,128)(2,1)}, u32[]{:S(2)}, u32[]{:S(2)}) collective-permute-start(bf16[16,128,128]{2,1,0:T(8,128)(2,1)} %fusion.27), channel_id=1, source_target_pairs={{0,32},{4,36},{8,40},{12,44},{16,48},{20,52},{24,56},{28,60},{32,6... | collective-permute-start | bytes 1572872 | tf_op jit(solution)/shard_map/ppermute | solution.py:15
  81.7 11.1 %collective-permute-start.5 = (bf16[16,128,128]{2,1,0:T(8,128)(2,1)}, bf16[16,128,128]{2,1,0:T(8,128)(2,1)}, u32[]{:S(2)}, u32[]{:S(2)}) collective-permute-start(bf16[16,128,128]{2,1,0:T(8,128)(2,1)} %fusion.68), channel_id=1, source_target_pairs={{0,64},{4,68},{8,72},{12,76},{16,80},{20,84},{24,88},{28,92},{32,9... | collective-permute-start | bytes 1572872 | tf_op jit(solution)/shard_map/ppermute | solution.py:15
  97.9 5.3 %copy-start.9 = (pred[128,4]{0,1:T(4,128)(4,1)S(1)}, pred[128,4]{0,1:T(4,128)(4,1)}, u32[]{:S(2)}) copy-start(pred[128,4]{0,1:T(4,128)(4,1)} %broadcast_compare_fusion) | copy-start | bytes 1540
  105.0 116.2 %all-gather.6.cloned.1.call-start = ((), (), s32[]{:S(2)}) async-start(), calls=%async_computation.4 | async-start | bytes 13369344 | tf_op jit(solution)/shard_map/all_gather | solution.py:108
  230.6 6.0 %copy-start.11 = (s32[32]{0:T(128)S(1)}, s32[32]{0:T(128)}, u32[]{:S(2)}) copy-start(s32[32]{0:T(128)} %eq.56) | copy-start | bytes 388
  232.1 28.8 %all-to-all-start = ((bf16[4,2,1,40,3072]{4,3,1,2,0:T(8,128)(2,1)}), bf16[4,2,1,40,3072]{4,3,1,2,0:T(8,128)(2,1)}, u32[]{:S(2)}, u32[]{:S(2)}) async-start(bf16[4,2,1,40,3072]{4,3,1,2,0:T(8,128)(2,1)} %pad_maximum_fusion), calls=%async_computation | async-start | bytes 3932160 | tf_op jit(solution)/shard_map/all_to_all | solution.py:113
  236.6 90.0 %all-gather.8.cloned.1.call-start = ((), (), s32[]{:S(2)}) async-start(), calls=%async_computation.5 | async-start | bytes 3244032 | tf_op jit(solution)/shard_map/all_gather | solution.py:135
  340.7 5.5 %copy-start.13 = (s32[128,2]{0,1:T(2,128)S(1)}, s32[128,2]{0,1:T(2,128)}, u32[]{:S(2)}) copy-start(s32[128,2]{0,1:T(2,128)} %param.23) | copy-start | bytes 3076
  340.7 5.5 %copy-start.14 = (f32[128,2]{0,1:T(2,128)S(1)}, f32[128,2]{0,1:T(2,128)}, u32[]{:S(2)}) copy-start(f32[128,2]{0,1:T(2,128)} %param.24) | copy-start | bytes 3076
  340.7 45.3 %all-to-all-start.2 = ((bf16[32,8,6144]{2,1,0:T(8,128)(2,1)}), bf16[32,8,6144]{2,1,0:T(8,128)(2,1)}, u32[]{:S(2)}, u32[]{:S(2)}) async-start(bf16[32,8,6144]{2,1,0:T(8,128)(2,1)} %fusion), calls=%async_computation.2 | async-start | bytes 6291456 | tf_op jit(solution)/shard_map/all_to_all | solution.py:140
  (2 other events, 4.5 us)
Sparse Core Ops, SparseCore 0:
  105.2 22.7 all-gather.3
  130.1 91.0 all-gather.5
  283.5 42.9 all-gather.7
